TPU v7x, 256 devices: a whole 4x4x8 slice. The times are simulated.
256 devices in a mesh: row: 32 (over y, x, core), col: 8 (over z).
Axes of the slice: x: 4, y: 4, z: 8, core: 2. Of those that a mesh axis runs over, the one named last changes fastest.
Arguments:
- head_points: float32 [8, 2, 1024], P(None, None, 'row'), may hold values from 0 to 1
- tail_points: float32 [8, 32768], P(None, 'row'), may hold values from 0 to 1
- eval_points: float32 [8, 8192], P(None, 'col'), may hold values from 0 to 1
- length_scales: float32 [8], replicated, may hold values from 0.5 to 2
- head_factor: float32 [2, 1024, 2, 1024], P(None, 'row', None, 'col'), as said below
- tail_factor: float32 [32768, 2, 1024], P('row', None, 'col'), may hold values from -0.125 to 0.125
Outputs:
- head_solved: float32 [2, 1024, 8192], P(None, 'row', 'col')
- tail_rhs: float32 [32768, 8192], P('row', 'col')
Inputs may be any that keep to these rules, and one draw needn't show every extreme that they name: head_factor[p, :, q, :] is zero for q > p; the blocks with p = q are lower triangular with a diagonal between 1 and 2.
All inputs are finite; a program needn't handle non-finite values.
Results may differ from a plain program's by a relative error of at most 0.00011.
Values sent between devices are 32-bit elements; how exact they have to be, the bound alone decides.
No kernel may reach another device: no remote copies, remote signals or barrier semaphores. Data moves between devices by JAX's collectives and lax.ppermute only.
A program may use at most 192 MiB of HBM per device.

v0:
```python
import jax
import jax.numpy as jnp
from jax import lax
from jax.sharding import PartitionSpec as P


def kernel_block(row_points, col_points, length_scales):
    total = jnp.zeros((row_points.shape[1], col_points.shape[1]), jnp.float32)
    for dimension in range(row_points.shape[0]):
        spread = (row_points[dimension][:, None] - col_points[dimension][None, :]) / length_scales[
            dimension
        ]
        total = total + spread * spread
    scaled = jnp.sqrt(5.0 * total)
    return (1.0 + scaled + scaled * scaled / 3.0) * jnp.exp(-scaled)


def whole_triangle(block):
    band = lax.all_gather(block, "col", axis=1, tiled=True)
    return lax.all_gather(band, "row", axis=0, tiled=True)


def solve_panel(block, right_side):
    triangle = whole_triangle(block)
    spread = lax.all_to_all(right_side, "row", split_axis=1, concat_axis=0, tiled=True)
    partial_value = jax.scipy.linalg.solve_triangular(triangle, spread, lower=True)
    return lax.all_gather(partial_value, "row", axis=1, tiled=True)


def apply_panel(rows_factor, solved):
    return jnp.dot(
        lax.all_gather(rows_factor, "col", axis=1, tiled=True),
        solved,
        precision=lax.Precision.HIGHEST,
        preferred_element_type=jnp.float32,
    )


def per_device(head_points, tail_points, eval_points, length_scales, head_factor, tail_factor):
    panel_rows = head_factor.shape[1]
    row_index = lax.axis_index("row")
    second = kernel_block(head_points[:, 1, :], eval_points, length_scales)
    tail = kernel_block(tail_points, eval_points, length_scales)
    first = kernel_block(head_points[:, 0, :], eval_points, length_scales)
    solved_one = solve_panel(head_factor[0, :, 0, :], first)
    update_rows = jnp.concatenate([head_factor[1, :, 0, :], tail_factor[:, 0, :]], 0)
    change = apply_panel(update_rows, solved_one)
    second_rhs = second - change[:panel_rows]
    tail = tail - change[panel_rows:]
    solved_two = solve_panel(head_factor[1, :, 1, :], second_rhs)
    tail = tail - apply_panel(tail_factor[:, 1, :], solved_two)
    local_one = lax.dynamic_slice_in_dim(solved_one, row_index * panel_rows, panel_rows, 0)
    local_two = lax.dynamic_slice_in_dim(solved_two, row_index * panel_rows, panel_rows, 0)
    return (jnp.stack([local_one, local_two]), tail)


def solution(mesh):
    placed = (
        P(None, None, "row"),
        P(None, "row"),
        P(None, "col"),
        P(),
        P(None, "row", None, "col"),
        P("row", None, "col"),
    )
    return jax.shard_map(
        per_device,
        mesh=mesh,
        in_specs=placed,
        out_specs=(P(None, "row", "col"), P("row", "col")),
        check_vma=False,
    )
```

profile of v0, /device:TPU:0, one launch (start us, length us, event | category | flops | bytes accessed | tf_op | source)
XLA Modules:
  0.0 561.0 jit_solution(13465957353782075579)
XLA Ops:
  8.1 28.5 %all-gather = f32[1,32,1,1024]{3,1,2,0:T(8,128)} all-gather(f32[1,32,1,128]{3,1,2,0:T(8,128)S(1)} %bitcast.220), channel_id=2, replica_groups=mesh['row'=32,'col'=8] {'col'}, dimensions={3}, use_global_device_ids=true | all-gather | bytes 147456 | tf_op jit(solution)/shard_map/all_gather | solution.py:19
  36.7 26.6 %all-gather.2 = f32[1,32,1,1024]{3,1,2,0:T(8,128)} all-gather(f32[1,32,1,128]{3,1,2,0:T(8,128)S(1)} %bitcast.219), channel_id=4, replica_groups=mesh['row'=32,'col'=8] {'col'}, dimensions={3}, use_global_device_ids=true | all-gather | bytes 147456 | tf_op jit(solution)/shard_map/all_gather | solution.py:19
  63.3 3.3 fusion.73
  68.9 6.2 %fusion.77 = f32[32,32,32]{2,1,0:T(8,128)S(1)} fusion(f32[]{:T(128)} %bitcast.17, f32[32,32]{1,0:T(8,128)S(1)} %sub.446, f32[32]{0:T(128)S(1)} %get-tuple-element.124, f32[]{:T(128)} %bitcast.15, f32[32,32]{1,0:T(8,128)S(1)} %sub.441, f32[32]{0:T(128)S(1)} %get-tuple-element.125, f32[]{:T(128)} %bitcast.13, f32[32,32]{1,0:T(8,128)S(1)} %sub.436, ...), kind=kLoop, calls=%fused_computation.196 | loop fusion | flops 1245184 | bytes 164896
  76.0 7.3 %all-to-all-start = ((f32[32,1,1024]{2,1,0:T(1,128)}), f32[32,1,1024]{2,1,0:T(1,128)S(1)}, u32[]{:S(2)}, u32[]{:S(2)}) async-start(f32[32,1,1024]{2,1,0:T(1,128)} %reshape.231), calls=%async_computation | async-start | bytes 262144 | tf_op jit(solution)/shard_map/all_to_all | solution.py:25
  83.4 7.7 %all-to-all-done = f32[32,1,1024]{2,1,0:T(1,128)S(1)} async-done(((f32[32,1,1024]{2,1,0:T(1,128)}), f32[32,1,1024]{2,1,0:T(1,128)S(1)}, u32[]{:S(2)}, u32[]{:S(2)}) %all-to-all-start) | async-done | bytes 131104 | tf_op jit(solution)/shard_map/all_to_all | solution.py:25
  93.5 4.8 bitcast_select_fusion.1
  98.3 24.1 %while.4 = (s32[]{:T(128)}, f32[1024,1024]{1,0:T(8,128)}, s32[8,2]{0,1:T(2,128)S(1)}, f32[8,128,128]{2,1,0:T(8,128)S(1)}, s32[]{:T(128)}) while((s32[]{:T(128)}, f32[1024,1024]{1,0:T(8,128)}, s32[8,2]{0,1:T(2,128)S(1)}, f32[8,128,128]{2,1,0:T(8,128)S(1)}, s32[]{:T(128)}) %tuple.131), condition=%wide.while_cond, body=%wide.while_body.sunk | while | flops 2 | bytes 131189 | solution.py:26
  99.0 2.3 bitcast_dynamic-update-slice_fusion.4
  102.0 2.3 bitcast_dynamic-update-slice_fusion.4
  105.0 2.3 bitcast_dynamic-update-slice_fusion.4
  108.0 2.3 bitcast_dynamic-update-slice_fusion.4
  111.1 2.3 bitcast_dynamic-update-slice_fusion.4
  114.1 2.3 bitcast_dynamic-update-slice_fusion.4
  117.1 2.3 bitcast_dynamic-update-slice_fusion.4
  120.1 2.3 bitcast_dynamic-update-slice_fusion.4
  122.4 78.6 %custom-call.4 = f32[8,128,128]{1,2,0:T(8,128)S(1)} custom-call(f32[8,128,128]{2,1,0:T(8,128)S(1)} %get-tuple-element.17), custom_call_target="InvertDiagBlocksLowerTriangular" | custom-call | tf_op jit(solution)/shard_map/jit(_solve_triangular)/triangular_solve | solution.py:26
  212.5 4.8 bitcast_select_fusion
  217.2 43.9 %all-gather.12.cloned.1.call-done = f32[1024,1024]{0,1:T(8,128)} async-done(((f32[1024,32]{0,1:T(8,128)}), f32[1024,1024]{0,1:T(8,128)}) %all-gather.12.cloned.1.call-update) | async-done | bytes 4194320 | tf_op jit(solution)/shard_map/all_gather | solution.py:27
  261.2 17.2 %fusion.78 = f32[1056,1024]{1,0:T(8,128)S(1)} fusion(f32[1056,1024]{1,0:T(8,128)} %all-gather.14.cloned.1.call-done, f32[1024,1024]{0,1:T(8,128)} %all-gather.12.cloned.1.call-done), kind=kOutput, calls=%fused_computation.199 | convolution fusion | flops 13287555072 | bytes 12845056 | tf_op jit(solution)/shard_map/dot_general | solution.py:31
  280.4 5.3 slice_subtract_fusion.1
  286.8 5.2 all-to-all-start.1
  292.2 22.5 %while.5 = (s32[]{:T(128)}, f32[1024,1024]{1,0:T(8,128)}, s32[8,2]{0,1:T(2,128)S(1)}, f32[8,128,128]{2,1,0:T(8,128)S(1)}, s32[]{:T(128)}) while((s32[]{:T(128)}, f32[1024,1024]{1,0:T(8,128)}, s32[8,2]{0,1:T(2,128)S(1)}, f32[8,128,128]{2,1,0:T(8,128)S(1)}, s32[]{:T(128)}) %tuple.149), condition=%wide.while_cond.clone, body=%wide.while_body.clone.sunk | while | flops 2 | bytes 131189 | solution.py:26
  292.8 2.2 bitcast_dynamic-update-slice_fusion.5
  295.6 2.2 bitcast_dynamic-update-slice_fusion.5
  298.5 2.2 bitcast_dynamic-update-slice_fusion.5
  301.3 2.2 bitcast_dynamic-update-slice_fusion.5
  304.1 2.2 bitcast_dynamic-update-slice_fusion.5
  314.7 78.6 %custom-call.5 = f32[8,128,128]{1,2,0:T(8,128)S(1)} custom-call(f32[8,128,128]{2,1,0:T(8,128)S(1)} %get-tuple-element.18), custom_call_target="InvertDiagBlocksLowerTriangular" | custom-call | tf_op jit(solution)/shard_map/jit(_solve_triangular)/triangular_solve | solution.py:26
  407.0 52.2 %all-gather.16.cloned.1.call-done = f32[1024,1024]{0,1:T(8,128)} async-done(((f32[1024,32]{0,1:T(8,128)}), f32[1024,1024]{0,1:T(8,128)}) %all-gather.16.cloned.1.call-update) | async-done | bytes 4194320 | tf_op jit(solution)/shard_map/all_gather | solution.py:27
  461.8 62.9 %all-gather.22.cloned.1.call-done = f32[1024,1,1024]{2,0,1:T(8,128)} async-done(((f32[1024,1,128]{2,0,1:T(8,128)}), f32[1024,1,1024]{2,0,1:T(8,128)}) %all-gather.22.cloned.1.call-update) | async-done | bytes 4194320 | tf_op jit(solution)/shard_map/all_gather | solution.py:32
  524.8 29.4 %fusion = f32[1024,1024]{1,0:T(8,128)} fusion(f32[1056,1024]{1,0:T(8,128)} %copy-done.6, f32[]{:T(128)} %bitcast.17, f32[1024]{0:T(1024)S(1)} %bitcast.236, f32[1024]{0:T(1024)S(1)} %bitcast.243, f32[]{:T(128)} %bitcast.15, f32[1024]{0:T(1024)S(1)} %bitcast.234, f32[1024]{0:T(1024)S(1)} %bitcast.244, f32[]{:T(128)} %bitcast.13, f32[1024]{0:T(1024)S(1)} %bitcast.232, ...), kind=kOutput, calls=%fused_computation.5 | convolution fusion | flops 12926844928 | bytes 16842784 | tf_op jit(solution)/shard_map/dot_general | solution.py:31
  (131 shorter events, 54.0 us)
Async XLA Ops:
  7.2 60.3 %copy-start.2 = (f32[8,1024]{1,0:T(8,128)S(1)}, f32[8,1024]{1,0:T(8,128)}, u32[]{:S(2)}) copy-start(f32[8,1024]{1,0:T(8,128)} %param.10) | copy-start | bytes 98308
  7.2 60.4 %copy-start.5 = (f32[8,2,32]{2,1,0:T(2,128)S(1)}, f32[8,2,32]{2,1,0:T(2,128)}, u32[]{:S(2)}) copy-start(f32[8,2,32]{2,1,0:T(2,128)} %param.8) | copy-start | bytes 6148
  7.2 60.5 %copy-start.4 = (f32[8]{0:T(128)S(1)}, f32[8]{0:T(128)}, u32[]{:S(2)}) copy-start(f32[8]{0:T(128)} %param.11) | copy-start | bytes 100
  7.2 86.3 %all-gather.18.cloned.1.call-start = ((), (), s32[]{:S(2)}) async-start(), calls=%async_computation.5 | async-start | bytes 4325376 | tf_op jit(solution)/shard_map/all_gather | solution.py:20
  36.6 175.9 %all-gather.20.cloned.1.call-start = ((), (), s32[]{:S(2)}) async-start(), calls=%async_computation.6 | async-start | bytes 4325376 | tf_op jit(solution)/shard_map/all_gather | solution.py:20
  63.3 154.0 %all-gather.14.cloned.1.call-start = ((), (), s32[]{:S(2)}) async-start(), calls=%async_computation.3 | async-start | bytes 4866048 | tf_op jit(solution)/shard_map/all_gather | solution.py:32
  76.0 15.1 %all-to-all-start = ((f32[32,1,1024]{2,1,0:T(1,128)}), f32[32,1,1024]{2,1,0:T(1,128)S(1)}, u32[]{:S(2)}, u32[]{:S(2)}) async-start(f32[32,1,1024]{2,1,0:T(1,128)} %reshape.231), calls=%async_computation | async-start | bytes 262144 | tf_op jit(solution)/shard_map/all_to_all | solution.py:25
  83.4 177.8 %all-gather.12.cloned.1.call-start = ((), (), s32[]{:S(2)}) async-start(), calls=%async_computation.2 | async-start | bytes 4325376 | tf_op jit(solution)/shard_map/all_gather | solution.py:27
  211.8 0.7 copy-start
  278.4 2.0 copy-start.6
  286.8 106.4 %all-to-all-start.1 = ((f32[32,1,1024]{2,1,0:T(1,128)}), f32[32,1,1024]{2,1,0:T(1,128)S(1)}, u32[]{:S(2)}, u32[]{:S(2)}) async-start(f32[32,1,1024]{2,1,0:T(1,128)} %reshape.233), calls=%async_computation.1 | async-start | bytes 262144 | tf_op jit(solution)/shard_map/all_to_all | solution.py:25
  292.1 167.1 %all-gather.16.cloned.1.call-start = ((), (), s32[]{:S(2)}) async-start(), calls=%async_computation.4 | async-start | bytes 4325376 | tf_op jit(solution)/shard_map/all_gather | solution.py:27
  314.7 92.3 %copy-start.3 = (f32[8,1024]{1,0:T(8,128)S(1)}, f32[8,1024]{1,0:T(8,128)}, u32[]{:S(2)}) copy-start(f32[8,1024]{1,0:T(8,128)} %param.9) | copy-start | bytes 98308
  405.7 0.7 copy-start.1
  406.4 118.4 %all-gather.22.cloned.1.call-start = ((), (), s32[]{:S(2)}) async-start(), calls=%async_computation.7 | async-start | bytes 4718592 | tf_op jit(solution)/shard_map/all_gather | solution.py:32
Sparse Core Ops, SparseCore 0:
  36.7 50.4 all-gather.17
  89.8 51.4 all-gather.19
  143.1 63.5 all-gather.13
  212.6 48.5 all-gather.11
  406.5 52.6 all-gather.15
  460.8 63.9 all-gather.21
where the time goes:
time: 563 us; the launch traced here: 561 us
  other arithmetic  182 us (32%)
  waiting for transfers between devices  167 us (30%)
  matrix products  67.7 us (12%)
  local copies, waits for them, and re-layouts  61.2 us (11%)
  blocking collectives  55 us (10%)
  between operations  14.6 us (3%)
  starting transfers between devices  12.8 us (2%)
    another operation x5, other arithmetic, solve_panel(): jax.scipy.linalg.solve_triangular(triangle, spread, lower=True)  167 us
    all_gather x2, waiting for transfers between devices, solve_panel(): return lax.all_gather(partial_value, 'row', axis=1, tiled=True)  96.1 us
    all_gather x2, waiting for transfers between devices, apply_panel(): lax.all_gather(rows_factor, 'col', axis=1, tiled=True)  62.9 us
    all_gather x2, blocking collectives, whole_triangle(): band = lax.all_gather(block, 'col', axis=1, tiled=True)  55 us
    dot_general x2, matrix products, apply_panel(): jnp.dot(lax.all_gather(rows_factor, 'col', axis=1, tiled=True), solved, p...  46.5 us
    another operation x51, local copies, waits for them, and re-layouts, solve_panel(): jax.scipy.linalg.solve_triangular(triangle, spread, lower=True)  46.4 us
    another operation x30, matrix products, solve_panel(): jax.scipy.linalg.solve_triangular(triangle, spread, lower=True)  21.2 us
    all_to_all x2, starting transfers between devices, solve_panel(): lax.all_to_all(right_side, 'row', split_axis=1, concat_axis=0, tiled=True)  12.6 us
  transfers between devices with their start and end apart: 8, of which 4 were waited for; matrix products, arithmetic and copies ran while one was open for 43% of the time, Pallas kernels for 0%

commit v1 on v0

--- a/solution.py
+++ b/solution.py
@@ -2,6 +2,16 @@
 import jax.numpy as jnp
 from jax import lax
 from jax.sharding import PartitionSpec as P
+
+render_limits = lambda sheet, group_axis, along_dim: jnp.concatenate(
+    lax.all_to_all(
+        jnp.stack([sheet for _ in range(lax.axis_size(group_axis))], 0),
+        axis_name=group_axis,
+        split_axis=0,
+        concat_axis=0,
+    ),
+    along_dim,
+)
 
 
 def kernel_block(row_points, col_points, length_scales):
@@ -24,7 +34,7 @@
     triangle = whole_triangle(block)
     spread = lax.all_to_all(right_side, "row", split_axis=1, concat_axis=0, tiled=True)
     partial_value = jax.scipy.linalg.solve_triangular(triangle, spread, lower=True)
-    return lax.all_gather(partial_value, "row", axis=1, tiled=True)
+    return render_limits(partial_value, "row", 1)
 
 
 def apply_panel(rows_factor, solved):

time: 563 us -> 528 us (0.938)
  the two profiles are of different devices: /device:TPU:0 before, /device:TPU:32 now
where the time goes in v1:
time: 528 us; the launch traced here: 518 us
  other arithmetic  181 us (34%)
  waiting for transfers between devices  94.8 us (18%)
  local copies, waits for them, and re-layouts  68.8 us (13%)
  matrix products  67.5 us (13%)
  blocking collectives  56 us (11%)
  starting transfers between devices  34.9 us (7%)
  between operations  14.6 us (3%)
    another operation x5, other arithmetic, solve_panel(): jax.scipy.linalg.solve_triangular(triangle, spread, lower=True)  167 us
    all_to_all x2, waiting for transfers between devices, lax.all_to_all(jnp.stack([sheet for _ in range(lax.axis_size(group_axis))...  91.1 us
    all_gather x2, blocking collectives, whole_triangle(): band = lax.all_gather(block, 'col', axis=1, tiled=True)  56 us
    another operation x51, local copies, waits for them, and re-layouts, solve_panel(): jax.scipy.linalg.solve_triangular(triangle, spread, lower=True)  47.3 us
    dot_general x2, matrix products, apply_panel(): jnp.dot(lax.all_gather(rows_factor, 'col', axis=1, tiled=True), solved, p...  46.3 us
    another operation x30, matrix products, solve_panel(): jax.scipy.linalg.solve_triangular(triangle, spread, lower=True)  21.2 us
    all_to_all x2, starting transfers between devices, lax.all_to_all(jnp.stack([sheet for _ in range(lax.axis_size(group_axis))...  12.7 us
    all_to_all x2, starting transfers between devices, solve_panel(): lax.all_to_all(right_side, 'row', split_axis=1, concat_axis=0, tiled=True)  11.2 us
  transfers between devices with their start and end apart: 8, of which 3 were waited for; matrix products, arithmetic and copies ran while one was open for 55% of the time, Pallas kernels for 0%

profile of v1, /device:TPU:32, one launch (start us, length us, event | category | flops | bytes accessed | tf_op | source)
XLA Modules:
  0.0 518.3 jit_solution(17880325209548639007)
XLA Ops:
  8.1 29.4 %all-gather = f32[1,32,1,1024]{3,1,2,0:T(8,128)} all-gather(f32[1,32,1,128]{3,1,2,0:T(8,128)S(1)} %bitcast.226), channel_id=2, replica_groups=mesh['row'=32,'col'=8] {'col'}, dimensions={3}, use_global_device_ids=true | all-gather | bytes 147456 | tf_op jit(solution)/shard_map/all_gather | solution.py:29
  37.5 26.6 %all-gather.2 = f32[1,32,1,1024]{3,1,2,0:T(8,128)} all-gather(f32[1,32,1,128]{3,1,2,0:T(8,128)S(1)} %bitcast.225), channel_id=4, replica_groups=mesh['row'=32,'col'=8] {'col'}, dimensions={3}, use_global_device_ids=true | all-gather | bytes 147456 | tf_op jit(solution)/shard_map/all_gather | solution.py:29
  68.4 6.1 %fusion.77 = f32[32,32,32]{2,1,0:T(8,128)S(1)} fusion(f32[]{:T(128)} %bitcast.17, f32[32,32]{1,0:T(8,128)S(1)} %sub.446, f32[32]{0:T(128)S(1)} %get-tuple-element.124, f32[]{:T(128)} %bitcast.15, f32[32,32]{1,0:T(8,128)S(1)} %sub.441, f32[32]{0:T(128)S(1)} %get-tuple-element.125, f32[]{:T(128)} %bitcast.13, f32[32,32]{1,0:T(8,128)S(1)} %sub.436, ...), kind=kLoop, calls=%fused_computation.196 | loop fusion | flops 1245184 | bytes 164896
  75.5 7.3 %all-to-all-start = ((f32[32,1,1024]{2,1,0:T(1,128)}), f32[32,1,1024]{2,1,0:T(1,128)S(1)}, u32[]{:S(2)}, u32[]{:S(2)}) async-start(f32[32,1,1024]{2,1,0:T(1,128)} %reshape.251), calls=%async_computation | async-start | bytes 262144 | tf_op jit(solution)/shard_map/all_to_all | solution.py:35
  82.9 3.3 fusion.73
  87.1 3.5 all-to-all-done
  92.9 4.8 bitcast_select_fusion.1
  97.7 24.2 %while.4 = (s32[]{:T(128)}, f32[1024,1024]{1,0:T(8,128)}, s32[8,2]{0,1:T(2,128)S(1)}, f32[8,128,128]{2,1,0:T(8,128)S(1)}, s32[]{:T(128)}) while((s32[]{:T(128)}, f32[1024,1024]{1,0:T(8,128)}, s32[8,2]{0,1:T(2,128)S(1)}, f32[8,128,128]{2,1,0:T(8,128)S(1)}, s32[]{:T(128)}) %tuple.131), condition=%wide.while_cond, body=%wide.while_body.sunk | while | flops 2 | bytes 131189 | solution.py:36
  98.4 2.3 bitcast_dynamic-update-slice_fusion.4
  101.4 2.3 bitcast_dynamic-update-slice_fusion.4
  104.5 2.3 bitcast_dynamic-update-slice_fusion.4
  107.5 2.3 bitcast_dynamic-update-slice_fusion.4
  110.5 2.3 bitcast_dynamic-update-slice_fusion.4
  113.6 2.3 bitcast_dynamic-update-slice_fusion.4
  116.6 2.3 bitcast_dynamic-update-slice_fusion.4
  121.9 78.6 %custom-call.4 = f32[8,128,128]{1,2,0:T(8,128)S(1)} custom-call(f32[8,128,128]{2,1,0:T(8,128)S(1)} %get-tuple-element.17), custom_call_target="InvertDiagBlocksLowerTriangular" | custom-call | tf_op jit(solution)/shard_map/jit(_solve_triangular)/triangular_solve | solution.py:36
  211.2 2.5 stack.10
  213.8 4.9 all-to-all-start.1
  218.7 10.9 %all-gather.16.cloned.1.call-start = ((), (), s32[]{:S(2)}) async-start(), calls=%async_computation.7 | async-start | bytes 4718592 | tf_op jit(solution)/shard_map/all_gather | solution.py:42
  229.6 4.7 bitcast_select_fusion
  234.3 37.9 %all-to-all-done.1 = f32[32,1024,32]{1,2,0:T(8,128)} async-done(((f32[32,1024,32]{1,2,0:T(8,128)}), f32[32,1024,32]{1,2,0:T(8,128)}, u32[]{:S(2)}, u32[]{:S(2)}) %all-to-all-start.1) | async-done | bytes 4194336 | tf_op jit(solution)/shard_map/all_to_all | solution.py:7
  272.1 17.2 %fusion.78 = f32[1056,1024]{1,0:T(8,128)S(1)} fusion(f32[1056,1024]{1,0:T(8,128)} %all-gather.10.cloned.1.call-done, f32[1024,1024]{0,1:T(8,128)} %bitcast.27), kind=kOutput, calls=%fused_computation.199 | convolution fusion | flops 13287555072 | bytes 12845056 | tf_op jit(solution)/shard_map/dot_general | solution.py:41
  291.3 5.3 %slice_subtract_fusion.1 = f32[32,1024]{1,0:T(8,128)S(1)} fusion(f32[1056,1024]{1,0:T(8,128)S(1)} %fusion.78, f32[]{:T(128)} %bitcast.17, f32[1024]{0:T(1024)S(1)} %bitcast.241, f32[32]{0:T(128)S(1)} %get-tuple-element.132, f32[]{:T(128)} %bitcast.15, f32[1024]{0:T(1024)S(1)} %bitcast.239, f32[32]{0:T(128)S(1)} %get-tuple-element.133, f32[]{:T(128)} %bitcast.13, ...), kind=kLoop, calls=%fused_computation.41 | loop fusion | flops 1277952 | bytes 295968 | tf_op jit(solution)/shard_map/sub | solution.py:58
  297.7 3.9 all-to-all-start.2
  301.6 23.4 %while.5 = (s32[]{:T(128)}, f32[1024,1024]{1,0:T(8,128)}, s32[8,2]{0,1:T(2,128)S(1)}, f32[8,128,128]{2,1,0:T(8,128)S(1)}, s32[]{:T(128)}) while((s32[]{:T(128)}, f32[1024,1024]{1,0:T(8,128)}, s32[8,2]{0,1:T(2,128)S(1)}, f32[8,128,128]{2,1,0:T(8,128)S(1)}, s32[]{:T(128)}) %tuple.145), condition=%wide.while_cond.clone, body=%wide.while_body.clone.sunk | while | flops 2 | bytes 131189 | solution.py:36
  302.3 2.3 bitcast_dynamic-update-slice_fusion.5
  314.0 2.3 bitcast_dynamic-update-slice_fusion.5
  325.0 78.6 %custom-call.5 = f32[8,128,128]{1,2,0:T(8,128)S(1)} custom-call(f32[8,128,128]{2,1,0:T(8,128)S(1)} %get-tuple-element.18), custom_call_target="InvertDiagBlocksLowerTriangular" | custom-call | tf_op jit(solution)/shard_map/jit(_solve_triangular)/triangular_solve | solution.py:36
  416.1 2.5 stack.12
  418.6 7.8 %all-to-all-start.3 = ((f32[32,1024,32]{1,2,0:T(8,128)}), f32[32,1024,32]{1,2,0:T(8,128)}, u32[]{:S(2)}, u32[]{:S(2)}) async-start(f32[32,1024,32]{1,2,0:T(8,128)} %stack.12), calls=%async_computation.3 | async-start | bytes 8388608 | tf_op jit(solution)/shard_map/all_to_all | solution.py:7
  426.5 53.2 %all-to-all-done.3 = f32[32,1024,32]{1,2,0:T(8,128)} async-done(((f32[32,1024,32]{1,2,0:T(8,128)}), f32[32,1024,32]{1,2,0:T(8,128)}, u32[]{:S(2)}, u32[]{:S(2)}) %all-to-all-start.3) | async-done | bytes 4194336 | tf_op jit(solution)/shard_map/all_to_all | solution.py:7
  482.4 29.0 %fusion = f32[1024,1024]{1,0:T(8,128)} fusion(f32[1056,1024]{1,0:T(8,128)} %copy-done.1, f32[]{:T(128)} %bitcast.17, f32[1024]{0:T(1024)S(1)} %bitcast.242, f32[1024]{0:T(1024)S(1)} %bitcast.249, f32[]{:T(128)} %bitcast.15, f32[1024]{0:T(1024)S(1)} %bitcast.240, f32[1024]{0:T(1024)S(1)} %bitcast.250, f32[]{:T(128)} %bitcast.13, f32[1024]{0:T(1024)S(1)} %bitcast.238, ...), kind=kOutput, calls=%fused_computation.5 | convolution fusion | flops 12926844928 | bytes 16842784 | tf_op jit(solution)/shard_map/dot_general | solution.py:41
  (121 shorter events, 64.4 us)
Async XLA Ops:
  7.2 85.7 %all-gather.12.cloned.1.call-start = ((), (), s32[]{:S(2)}) async-start(), calls=%async_computation.5 | async-start | bytes 4325376 | tf_op jit(solution)/shard_map/all_gather | solution.py:30
  37.5 192.1 %all-gather.14.cloned.1.call-start = ((), (), s32[]{:S(2)}) async-start(), calls=%async_computation.6 | async-start | bytes 4325376 | tf_op jit(solution)/shard_map/all_gather | solution.py:30
  75.5 15.1 %all-to-all-start = ((f32[32,1,1024]{2,1,0:T(1,128)}), f32[32,1,1024]{2,1,0:T(1,128)S(1)}, u32[]{:S(2)}, u32[]{:S(2)}) async-start(f32[32,1,1024]{2,1,0:T(1,128)} %reshape.251), calls=%async_computation | async-start | bytes 262144 | tf_op jit(solution)/shard_map/all_to_all | solution.py:35
  82.8 151.5 %all-gather.10.cloned.1.call-start = ((), (), s32[]{:S(2)}) async-start(), calls=%async_computation.4 | async-start | bytes 4866048 | tf_op jit(solution)/shard_map/all_gather | solution.py:42
  213.8 58.4 %all-to-all-start.1 = ((f32[32,1024,32]{1,2,0:T(8,128)}), f32[32,1024,32]{1,2,0:T(8,128)}, u32[]{:S(2)}, u32[]{:S(2)}) async-start(f32[32,1024,32]{1,2,0:T(8,128)} %stack.10), calls=%async_computation.1 | async-start | bytes 8388608 | tf_op jit(solution)/shard_map/all_to_all | solution.py:7
  218.7 263.7 %all-gather.16.cloned.1.call-start = ((), (), s32[]{:S(2)}) async-start(), calls=%async_computation.7 | async-start | bytes 4718592 | tf_op jit(solution)/shard_map/all_gather | solution.py:42
  289.4 2.0 copy-start.1
  297.7 105.9 %all-to-all-start.2 = ((f32[32,1,1024]{2,1,0:T(1,128)}), f32[32,1,1024]{2,1,0:T(1,128)S(1)}, u32[]{:S(2)}, u32[]{:S(2)}) async-start(f32[32,1,1024]{2,1,0:T(1,128)} %reshape.253), calls=%async_computation.2 | async-start | bytes 262144 | tf_op jit(solution)/shard_map/all_to_all | solution.py:35
  418.6 7.8 %copy-start = (f32[8,1024]{1,0:T(8,128)S(1)}, f32[8,1024]{1,0:T(8,128)}, u32[]{:S(2)}) copy-start(f32[8,1024]{1,0:T(8,128)} %param.9) | copy-start | bytes 98308
  418.6 61.1 %all-to-all-start.3 = ((f32[32,1024,32]{1,2,0:T(8,128)}), f32[32,1024,32]{1,2,0:T(8,128)}, u32[]{:S(2)}, u32[]{:S(2)}) async-start(f32[32,1024,32]{1,2,0:T(8,128)} %stack.12), calls=%async_computation.3 | async-start | bytes 8388608 | tf_op jit(solution)/shard_map/all_to_all | solution.py:7
Sparse Core Ops, SparseCore 0:
  37.6 51.3 all-gather.11
  91.6 51.5 all-gather.13
  144.9 63.2 all-gather.9
  229.7 63.1 all-gather.15
